TPU v7x, 32 devices: a whole 2x2x4 slice. The times are simulated.
32 devices in a mesh: grp: 4 (over y, core), dom: 8 (over z, x).
Axes of the slice: x: 2, y: 2, z: 4, core: 2. Of those that a mesh axis runs over, the one named last changes fastest.
Arguments:
- coarse: float32 [4096, 128], P(('grp', 'dom')), may hold values from -254 to 104
- region_map: int32 [131072], P(('grp', 'dom')), may hold values from 0 to 1023
- features: bfloat16 [32, 131072], P(None, ('grp', 'dom')), may hold values from 0 to 1
- reward_weights: float32 [32], replicated, may hold values from -1 to 1
- transitions: bfloat16 [1024, 8, 128, 128], P(('grp', 'dom')), may hold values from 4.9829483e-05 to 0.0009994507
- successors: int32 [1024, 8], P(('grp', 'dom')), may hold values from 0 to 39, as said below
- part_sizes: int32 [32], P(('grp', 'dom')), may hold values from 16 to 32, as said below
- outgoing_block_list: int32 [32, 8, 1], P(('grp', 'dom')), may hold values from 0 to 31, as said below
- destinations: int32 [128], replicated, may hold values from 0 to 131071, as said below
- anchors: bfloat16 [131072, 128], P(('grp', 'dom')), may hold values from 0.099609375 to 1
Outputs:
- values: bfloat16 [131072, 128], P(('grp', 'dom'))
- visits: bfloat16 [131072, 128], P(('grp', 'dom'))
- feature_counts: float32 [32, 128], replicated
Inputs may be any that keep to these rules, and one draw needn't show every extreme that they name: `successors`: entry 0 of a block's row is the block itself; entries 1 to 4 are blocks below the device's partition size; the last 3 entries are 32 or more and name received slots. `part_sizes`: some device holds 32 blocks. `outgoing_block_list`: every entry is below the sending device's partition size. `destinations`: each is a state of a block below its device's partition size.
All inputs are finite; a program needn't handle non-finite values.
Results may differ from a plain program's by a relative error of at most 0.0014.
The roundings to bfloat16 on the way count: a program that leaves them out, or rounds other values in their place, can miss the bound.
Values may be sent and summed in bfloat16 or wider, within the bound.
No kernel may reach another device: no remote copies, remote signals or barrier semaphores. Data moves between devices by JAX's collectives and lax.ppermute only.
A program may use at most 128 MiB of HBM per device.

v0:
```python
import jax
import jax.numpy as jnp
from jax import lax
from jax.experimental import pallas as pl
from jax.experimental.pallas import tpu as pltpu
from jax.sharding import PartitionSpec as P

ITERS = 3
VISITS = 3
REMOTE = 3
EXTRA = 16
UNIT = 8
ANY = pl.BlockSpec(memory_space=pltpu.HBM)
VMEM = pl.BlockSpec(memory_space=pltpu.VMEM)
SMEM = pl.BlockSpec(memory_space=pltpu.SMEM)
F32 = jnp.float32
BF16 = jnp.bfloat16
I32 = jnp.int32


def sds(shape, dtype):
    return jax.ShapeDtypeStruct(tuple(shape), dtype)


def mm(a, b):
    return jnp.dot(a, b, preferred_element_type=F32)


def mm_t(a, b):
    return lax.dot_general(a, b, (((0,), (0,)), ((), ())), preferred_element_type=F32)


def call(body, ins, outs, scratch, mib, flops, nbytes, name):
    return pl.pallas_call(
        body,
        out_shape=tuple(sds(shape, dtype) for _, shape, dtype in outs),
        in_specs=list(ins),
        out_specs=tuple(space for space, _, _ in outs),
        scratch_shapes=scratch,
        compiler_params=pltpu.CompilerParams(vmem_limit_bytes=mib << 20),
        cost_estimate=pl.CostEstimate(flops=flops, bytes_accessed=nbytes, transcendentals=0),
        name=name,
    )


def divisor(n, most):
    while n % most:
        most -= 1
    return most


def in_units(n, fn, before=None):
    step = divisor(n, UNIT)

    def turn(g):
        if before is not None:
            before(g)
        for i in range(step):
            fn(g * step + i)

    if n == step:
        turn(0)
        return

    @pl.loop(0, n // step)
    def _(g):
        turn(g)


def scale_rows(tops):
    peak = tops[0]
    for t in tops[1:]:
        peak = jnp.maximum(peak, t)
    return peak, [jnp.exp(t - peak) for t in tops]


def weigh(values):
    wide = values.astype(F32)
    top = jnp.max(wide, axis=0, keepdims=True)
    return jnp.exp(wide - top).astype(BF16), top


class Copies:
    def __init__(self, sem):
        self.sem, self.used = sem, 0

    def add(self, src, dst):
        at = self.used
        self.used += 1
        copy = pltpu.make_async_copy(src, dst, self.sem.at[at])
        copy.start()
        return copy


def make_kernels(nb, nsucc, s, d, slots, n_dom, rdev):
    local = nsucc - REMOTE
    nl = nb + slots
    per_peer = slots // n_dom
    blk = s * d
    pair = 2 * s * s * d
    step = divisor(nb, UNIT)
    turns = nb // step
    rows = nl + nb
    at_succ = 4
    at_listed = at_succ + nb * nsucc
    at_lead = at_listed + slots
    at_owner = at_lead + slots
    at_free = at_owner + slots

    def const_spec():
        return pltpu.VMEM((s + 8, 128), F32)

    def sems(n):
        return pltpu.SemaphoreType.DMA((n,))

    def new_values(backed, b, cst):
        sub = lax.broadcasted_iota(I32, (s, d), 0).astype(F32)
        here = sub == (cst[s : s + 1] - lax.convert_element_type(b * s, F32))
        lane = lax.broadcasted_iota(I32, (s, 128), 1)
        reward = jnp.sum(jnp.where(lane == b, cst[0:s], 0.0), axis=1, keepdims=True)
        return jnp.where(here, 0.0, reward + backed).astype(BF16)

    def chunks(sem, row, parts):
        def at(g, i):
            src, dst = parts[i](pl.ds(g * step, step))
            return pltpu.make_async_copy(src, dst, sem.at[row + i, g])

        def start(g):
            for i in range(len(parts)):
                at(g, i).start()

        def wait(g):
            for i in range(len(parts)):
                at(g, i).wait()

        return start, wait

    def start_all(start):
        for g in range(turns):
            start(g)

    def wait_all(wait):
        for g in range(turns):
            wait(g)

    def t_part(t_hbm, t_ref, k0, k1):
        return lambda at: (t_hbm.at[at, pl.ds(k0, k1 - k0)], t_ref.at[at])

    def in_part(src, dst):
        return lambda at: (src.at[at], dst.at[at])

    def pack_body(info, coarse, reg, out):
        table = coarse[...].astype(BF16)
        row = lax.broadcasted_iota(I32, (EXTRA, s), 0)
        for i in range(n_dom):
            out[i, 0:rdev] = table
            for j in range(per_peer):
                b = info[at_listed + i * per_peer + j]
                r = reg[pl.ds(b, 1)]
                high = lax.shift_right_logical(r, 7)
                low = jnp.bitwise_and(r, 127)
                extra = jnp.where(row == 0, high, jnp.where(row == 1, low, b))
                out[i, rdev + j * EXTRA : rdev + (j + 1) * EXTRA] = extra.astype(F32).astype(BF16)

    pack = call(
        pack_body, [SMEM, VMEM, VMEM],
        [(VMEM, (n_dom, rdev + per_peer * EXTRA, d), BF16)],
        [], 8, blk, 1 << 20, "pack",
    )

    def begin_body(
        info, rec, reg, cst_hbm, t_hbm, w_out, top_out, sent,
        w0, top0, table, regs, regs_t, where_d, cst, t_ref, sem, t_sem,
    ):
        cps = Copies(sem)
        got_cst = cps.add(cst_hbm, cst)
        for i in range(slots):
            pltpu.make_async_copy(t_hbm.at[info[at_listed + i]], t_ref.at[i], t_sem.at[i]).start()
        for i in range(n_dom):
            table[i * rdev : (i + 1) * rdev] = rec[i, 0:rdev]
        regs[...] = jnp.zeros_like(regs)
        regs[0:nb] = reg[...].astype(F32)
        got_cst.wait()
        own_d = cst[s : s + 1]
        for b in range(nb):
            where_d[b : b + 1] = own_d - float(b * s)
        for i in range(n_dom):
            for j in range(per_peer):
                k = nb + i * per_peer + j
                extra = rec[i, rdev + j * EXTRA : rdev + (j + 1) * EXTRA].astype(F32)
                regs[k : k + 1] = extra[0:1] * 128.0 + extra[1:2]
                shift = lax.convert_element_type(info[0] - (info[1] + i) * (nb * s), F32)
                where_d[k : k + 1] = own_d + shift - extra[2:3] * float(s)
        regs_t[...] = regs[...].T
        group = divisor(nl, 4)

        @pl.loop(0, nl // group)
        def _(g):
            lane_k = lax.broadcasted_iota(I32, (s, 128), 1)
            lane_f = lax.broadcasted_iota(I32, (s, rdev), 1).astype(F32)
            sub = lax.broadcasted_iota(I32, (s, d), 0).astype(F32)
            hot = []
            for u in range(group):
                col = jnp.sum(
                    jnp.where(lane_k == g * group + u, regs_t[...], 0.0), axis=1, keepdims=True
                )
                hot.append(
                    jnp.concatenate(
                        [
                            jnp.where(lane_f == (col - float(c * rdev)), 1.0, 0.0).astype(BF16)
                            for c in range(n_dom)
                        ],
                        axis=1,
                    )
                )
            picked = mm(jnp.concatenate(hot, axis=0), table[...])
            for u in range(group):
                k = g * group + u
                here = sub == where_d[pl.ds(k, 1)]
                w, top = weigh(jnp.where(here, 0.0, picked[u * s : (u + 1) * s]))
                w0[k] = w
                top0[pl.ds(k, 1)] = top

        put_w = cps.add(w0, w_out)
        put_top = cps.add(top0, top_out)
        for i in range(slots):
            pltpu.make_async_copy(t_hbm.at[info[at_listed + i]], t_ref.at[i], t_sem.at[i]).wait()

        def one(i):
            b = info[at_listed + i]
            peak, acc = all_terms(b, info, lambda k: t_ref[i, k], w0, top0)
            sent[i] = new_values(peak + jnp.log(acc), b, cst)

        in_units(slots, one)
        put_w.wait()
        put_top.wait()

    def all_terms(b, info, t_of, w_ref, top_ref, count=nsucc):
        es = [info[at_succ + b * nsucc + k] for k in range(count)]
        peak, sc = scale_rows([top_ref[pl.ds(e, 1)] for e in es])
        acc = mm(t_of(0), w_ref[es[0]]) * sc[0]
        for k in range(1, count):
            acc = acc + mm(t_of(k), w_ref[es[k]]) * sc[k]
        return peak, acc

    def remote_terms(b, info, t_of, w_ref, top_ref, peak0, acc0):
        es = [info[at_succ + b * nsucc + local + k] - nb for k in range(REMOTE)]
        peak, sc = scale_rows([peak0] + [top_ref[pl.ds(e, 1)] for e in es])
        acc = acc0 * sc[0]
        for k in range(REMOTE):
            acc = acc + mm(t_of(k), w_ref[es[k]]) * sc[k + 1]
        return peak, acc

    begin = call(
        begin_body, [SMEM, VMEM, VMEM, ANY, ANY],
        [(ANY, (nl, s, d), BF16), (ANY, (nl, d), F32), (VMEM, (slots, s, d), BF16)],
        [
            pltpu.VMEM((nl, s, d), BF16), pltpu.VMEM((nl, d), F32),
            pltpu.VMEM((n_dom * rdev, d), BF16), pltpu.VMEM((128, s), F32),
            pltpu.VMEM((s, 128), F32), pltpu.VMEM((nl, d), F32), const_spec(),
            pltpu.VMEM((slots, nsucc, s, s), BF16), sems(3), sems(slots),
        ],
        32, 2 * nl * s * n_dom * rdev * d + slots * nsucc * pair, 4 << 20, "begin",
    )

    def finish_local(info, t_ref, w_ref, top_ref, acc, peak, accl, acc_out, peak_out, put, sem, n0):
        def two(b):
            top, a = all_terms(b, info, lambda k: t_ref[b, k], w_ref, top_ref, local)
            acc[b] = a
            peak[pl.ds(b, 1)] = top

        def before(g):
            @pl.when(g > 0)
            def _():
                put(g - 1)

        in_units(nb, two, before)
        put(turns - 1)
        put_peak = pltpu.make_async_copy(peak, peak_out, sem.at[n0])
        put_peak.start()
        for i in range(slots):
            b = info[at_listed + i]
            accl[i, 0:s] = acc[b]
            accl[i, s : s + 8] = jnp.broadcast_to(peak[pl.ds(b, 1)], (8, d))
        put_peak.wait()

    def sweep_first_body(
        info, cst_hbm, t_hbm, w_hbm, top_hbm, acc_out, peak_out, accl,
        cst, t_ref, w0, top0, w1, top1, acc, peak, sem, c_sem,
    ):
        cps = Copies(sem)
        early = [cps.add(w_hbm, w0), cps.add(top_hbm, top0), cps.add(cst_hbm, cst)]
        start, wait = chunks(c_sem, 0, [t_part(t_hbm, t_ref, 0, nsucc)])
        put, put_wait = chunks(c_sem, 1, [lambda at: (acc.at[at], acc_out.at[at])])
        start_all(start)
        for c in early:
            c.wait()

        def one(b):
            top_all, a = all_terms(b, info, lambda k: t_ref[b, k], w0, top0)
            w, top = weigh(new_values(top_all + jnp.log(a), b, cst))
            w1[b] = w
            top1[pl.ds(b, 1)] = top

        in_units(nb, one, wait)
        finish_local(info, t_ref, w1, top1, acc, peak, accl, acc_out, peak_out, put, sem, 3)
        wait_all(put_wait)

    sweep_first = call(
        sweep_first_body, [SMEM, ANY, ANY, ANY, ANY],
        [(ANY, (nb, s, d), F32), (ANY, (nb, d), F32), (VMEM, (slots, s + 8, d), F32)],
        [
            const_spec(), pltpu.VMEM((nb, nsucc, s, s), BF16),
            pltpu.VMEM((nl, s, d), BF16), pltpu.VMEM((nl, d), F32),
            pltpu.VMEM((nb, s, d), BF16), pltpu.VMEM((nb, d), F32),
            pltpu.VMEM((nb, s, d), F32), pltpu.VMEM((nb, d), F32),
            sems(4), pltpu.SemaphoreType.DMA((2, turns)),
        ],
        40, nb * (nsucc + local) * pair, 12 << 20, "sweep_first",
    )

    def listed_next_body(info, got, accl, cst_hbm, t_hbm, sent, wr_out, cst, t_ref, topr, sem, t_sem):
        cps = Copies(sem)
        got_cst = cps.add(cst_hbm, cst)

        def cp(i):
            return pltpu.make_async_copy(
                t_hbm.at[info[at_listed + i], pl.ds(local, REMOTE)], t_ref.at[i], t_sem.at[i]
            )

        for i in range(slots):
            cp(i).start()
        for i in range(slots):
            w, top = weigh(got[i])
            wr_out[i, 0:s] = w
            wr_out[i, s : s + 16] = jnp.broadcast_to(top, (16, d)).astype(BF16)
            topr[i : i + 1] = top
        got_cst.wait()
        for i in range(slots):
            cp(i).wait()

        def one(i):
            b = info[at_listed + i]
            wr = WeightView(wr_out, s)
            peak, acc = remote_terms(
                b, info, lambda k: t_ref[i, k], wr, topr, accl[i, s : s + 1], accl[i, 0:s]
            )
            sent[i] = new_values(peak + jnp.log(acc), b, cst)

        in_units(slots, one)

    listed_next = call(
        listed_next_body, [SMEM, VMEM, VMEM, ANY, ANY],
        [(VMEM, (slots, s, d), BF16), (VMEM, (slots, s + 16, d), BF16)],
        [
            const_spec(), pltpu.VMEM((slots, REMOTE, s, s), BF16), pltpu.VMEM((slots, d), F32),
            sems(1), sems(slots),
        ],
        16, slots * REMOTE * pair, 3 << 20, "listed_next",
    )

    def sweep_next_body(
        info, wr, cst_hbm, t_hbm, acc_hbm, peak_hbm, w_out, top_out, acc_out, peak_out, wl_out,
        cst, t_ref, acc_in, peak_in, w2, top2, topr, acc, peak, accl, sem, c_sem,
    ):
        cps = Copies(sem)
        early = [cps.add(cst_hbm, cst), cps.add(peak_hbm, peak_in)]
        start, wait = chunks(
            c_sem, 0, [t_part(t_hbm, t_ref, 0, nsucc), in_part(acc_hbm, acc_in)]
        )
        put_w, put_w_wait = chunks(c_sem, 2, [lambda at: (w2.at[at], w_out.at[at])])
        put, put_wait = chunks(c_sem, 3, [lambda at: (acc.at[at], acc_out.at[at])])
        start_all(start)
        for i in range(slots):
            topr[i : i + 1] = wr[i, s : s + 1].astype(F32)
        for c in early:
            c.wait()

        def one(b):
            top_all, a = remote_terms(
                b, info, lambda k: t_ref[b, local + k], WeightView(wr, s), topr,
                peak_in[pl.ds(b, 1)], acc_in[b],
            )
            w, top = weigh(new_values(top_all + jnp.log(a), b, cst))
            w2[b] = w
            top2[pl.ds(b, 1)] = top

        in_units(nb, one, wait)
        start_all(put_w)
        put_top = cps.add(top2, top_out)
        finish_local(info, t_ref, w2, top2, acc, peak, accl, acc_out, peak_out, put, sem, 3)
        for i in range(slots):
            wl_out[i] = w2[info[at_listed + i]]
        put_top.wait()
        wait_all(put_w_wait)
        wait_all(put_wait)

    sweep_next = call(
        sweep_next_body, [SMEM, VMEM, ANY, ANY, ANY, ANY],
        [
            (ANY, (nb, s, d), BF16), (ANY, (nb, d), F32), (ANY, (nb, s, d), F32),
            (ANY, (nb, d), F32), (VMEM, (slots, s, d), BF16),
        ],
        [
            const_spec(), pltpu.VMEM((nb, nsucc, s, s), BF16),
            pltpu.VMEM((nb, s, d), F32), pltpu.VMEM((nb, d), F32),
            pltpu.VMEM((nb, s, d), BF16), pltpu.VMEM((nb, d), F32), pltpu.VMEM((slots, d), F32),
            pltpu.VMEM((nb, s, d), F32), pltpu.VMEM((nb, d), F32),
            pltpu.VMEM((slots, s + 8, d), F32),
            sems(4), pltpu.SemaphoreType.DMA((4, turns)),
        ],
        40, nb * nsucc * pair, 14 << 20, "sweep_next",
    )

    def add_flows(b, r, info, t_of, k0, k1, row, acc, base):
        peak = row[pl.ds(nl + b, 1)]
        for k in range(k0, k1):
            e = info[at_succ + b * nsucc + k]
            sc = jnp.exp(row[pl.ds(e, 1)] - peak)
            acc[e - base] = acc[e - base] + mm_t(t_of(k - k0), r) * sc

    def last_body(
        info, got, cst_hbm, t_hbm, acc_hbm, peak_hbm, top_hbm, anc_hbm,
        val_out, inv_out, r_out, row_out, sent, invl,
        cst, t_ref, acc_in, peak_in, row, anc, val, inv, r, wr, topr, slot_acc, sem, c_sem,
    ):
        cps = Copies(sem)
        early = [
            cps.add(cst_hbm, cst), cps.add(peak_hbm, peak_in), cps.add(top_hbm, row.at[pl.ds(0, nb)])
        ]
        start, wait = chunks(
            c_sem, 0,
            [t_part(t_hbm, t_ref, local, nsucc), in_part(acc_hbm, acc_in), in_part(anc_hbm, anc)],
        )
        put, put_wait = chunks(
            c_sem, 3,
            [in_part(val, val_out), in_part(inv, inv_out), in_part(r, r_out)],
        )
        start_all(start)
        slot_acc[...] = jnp.zeros_like(slot_acc)
        for i in range(slots):
            w, top = weigh(got[i])
            wr[i] = w
            topr[i : i + 1] = top
        for c in early:
            c.wait()
        row[nb:nl] = topr[...]

        def one(b):
            top_all, a = remote_terms(
                b, info, lambda k: t_ref[b, k], wr, topr, peak_in[pl.ds(b, 1)], acc_in[b]
            )
            row[pl.ds(nl + b, 1)] = top_all
            live = b < info[2]
            v = new_values(top_all + jnp.log(a), b, cst)
            val[b] = jnp.where(live, v.astype(F32), 0.0).astype(BF16)
            share = jnp.where(live, 1.0 / a, 0.0)
            inv[b] = share
            r[b] = (anc[b].astype(F32) * share).astype(BF16)

        in_units(nb, one, wait)
        start_all(put)
        put_row = cps.add(row, row_out)

        def two(b):
            add_flows(b, r[b], info, lambda k: t_ref[b, k], local, nsucc, row, slot_acc, nb)

        in_units(nb, two)
        sent[...] = slot_acc[...].astype(BF16)
        for i in range(slots):
            invl[i] = inv[info[at_listed + i]]
        put_row.wait()
        wait_all(put_wait)

    last = call(
        last_body, [SMEM, VMEM, ANY, ANY, ANY, ANY, ANY, ANY],
        [
            (ANY, (nb, s, d), BF16), (ANY, (nb, s, d), F32), (ANY, (nb, s, d), BF16),
            (ANY, (rows, d), F32), (VMEM, (slots, s, d), BF16), (VMEM, (slots, s, d), F32),
        ],
        [
            const_spec(), pltpu.VMEM((nb, REMOTE, s, s), BF16),
            pltpu.VMEM((nb, s, d), F32), pltpu.VMEM((nb, d), F32), pltpu.VMEM((rows, d), F32),
            pltpu.VMEM((nb, s, d), BF16), pltpu.VMEM((nb, s, d), BF16),
            pltpu.VMEM((nb, s, d), F32), pltpu.VMEM((nb, s, d), BF16),
            pltpu.VMEM((slots, s, d), BF16), pltpu.VMEM((slots, d), F32),
            pltpu.VMEM((slots, s, d), F32),
            sems(4), pltpu.SemaphoreType.DMA((6, turns)),
        ],
        40, nb * 2 * REMOTE * pair, 14 << 20, "last",
    )

    def make_spread(first, final):
        ks = local if final else nsucc

        def body(*refs):
            refs = list(refs)
            info = refs.pop(0)
            r_listed = None if first else refs.pop(0)
            row_hbm, t_hbm, r_hbm, w_hbm = refs[:4]
            refs = refs[4:]
            inv_hbm = None if final else refs.pop(0)
            total_hbm = None if first else refs.pop(0)
            if final:
                vis_out, totl = refs[:2]
                refs = refs[2:]
            else:
                total_out, r_out, ownl, part = refs[:4]
                refs = refs[4:]
            row, t_ref, r_in, w2, total, own, sem, c_sem = refs[:8]
            refs = refs[8:]
            if final:
                vis = refs.pop(0)
            else:
                inv, r_next = refs
            get_row = pltpu.make_async_copy(row_hbm, row, sem.at[0])
            get_row.start()
            start, wait = chunks(c_sem, 0, [t_part(t_hbm, t_ref, 0, ks)])
            r_start, r_wait = chunks(c_sem, 1, [in_part(r_hbm, r_in)])
            later = [in_part(w_hbm, w2)]
            if not final:
                later.append(in_part(inv_hbm, inv))
            if not first:
                later.append(in_part(total_hbm, total))
            late_start, late_wait = chunks(c_sem, 2, later)
            if final:
                out_parts = [in_part(vis, vis_out)]
            else:
                out_parts = [in_part(own if first else total, total_out), in_part(r_next, r_out)]
            put, put_wait = chunks(c_sem, 5, out_parts)
            start_all(r_start)
            start_all(start)
            start_all(late_start)
            own[...] = jnp.zeros_like(own)
            wait_all(r_wait)
            if not first:
                for i in range(slots):
                    @pl.when(info[at_lead + i] == 1)
                    def _(i=i):
                        r_in[info[at_listed + i]] = r_listed[i]
            get_row.wait()

            def one(b):
                add_flows(b, r_in[b], info, lambda k: t_ref[b, k], 0, local, row, own, 0)

            in_units(nb, one, wait)
            if not final:
                part[...] = jnp.zeros_like(part)

            def before(g):
                late_wait(g)

                @pl.when(g > 0)
                def _():
                    put(g - 1)

            def two(b):
                if final:
                    sums = total[b] + own[b]
                    own[b] = sums
                    mass = jnp.where(b < info[2], w2[b].astype(F32) * sums, 0.0)
                    vis[b] = mass.astype(BF16)
                    return
                free = lax.convert_element_type(info[at_free + b], F32)
                r = (w2[b].astype(F32) * own[b] * (inv[b] * free)).astype(BF16)
                r_next[b] = r
                if not first:
                    total[b] = total[b] + own[b]
                add_flows(b, r, info, lambda k: t_ref[b, local + k], local, nsucc, row, part, nb)

            in_units(nb, two, before)
            put(turns - 1)
            for i in range(slots):
                if final:
                    totl[i] = own[info[at_listed + i]]
                else:
                    ownl[i] = own[info[at_listed + i]]
            wait_all(put_wait)

        if final:
            outs = [(ANY, (nb, s, d), BF16), (VMEM, (slots, s, d), F32)]
        else:
            outs = [
                (ANY, (nb, s, d), F32), (ANY, (nb, s, d), BF16),
                (VMEM, (slots, s, d), F32), (VMEM, (slots, s, d), F32),
            ]
        ins = [SMEM] + ([] if first else [VMEM]) + [ANY] * 4
        ins += ([] if final else [ANY]) + ([] if first else [ANY])
        scratch = [
            pltpu.VMEM((rows, d), F32), pltpu.VMEM((nb, ks, s, s), BF16),
            pltpu.VMEM((nb, s, d), BF16), pltpu.VMEM((nb, s, d), BF16),
            pltpu.VMEM((nb, s, d), F32), pltpu.VMEM((nb, s, d), F32),
            sems(1), pltpu.SemaphoreType.DMA((7, turns)),
        ]
        if final:
            scratch.append(pltpu.VMEM((nb, s, d), BF16))
        else:
            scratch += [pltpu.VMEM((nb, s, d), F32), pltpu.VMEM((nb, s, d), BF16)]
        return call(body, ins, outs, scratch, 40, nb * ks * pair, 14 << 20, "spread")

    def make_join(first):
        def body(*refs):
            refs = list(refs)
            info, got, ownl, invl, wl, part, row_hbm, t_hbm = refs[:8]
            refs = refs[8:]
            back_in = None if first else refs.pop(0)
            sent, r_out, back, row, t_ref, sem, t_sem = refs

            def cp(i):
                return pltpu.make_async_copy(
                    t_hbm.at[info[at_listed + i], pl.ds(local, REMOTE)], t_ref.at[i], t_sem.at[i]
                )

            get_row = pltpu.make_async_copy(row_hbm, row, sem.at[0])
            get_row.start()
            for i in range(slots):
                cp(i).start()
            add_returned(info, got, back)
            get_row.wait()
            for i in range(slots):
                cp(i).wait()
            acc = part

            def one(i):
                b = info[at_listed + i]
                here = back[i]
                leads = lax.convert_element_type(info[at_lead + i], F32)
                mass = wl[i].astype(F32) * (ownl[i] + here)
                r_out[i] = (mass * (invl[i] * leads)).astype(BF16)
                if not first:
                    back[i] = back_in[i] + here

            in_units(slots, one)
            total = [None] * slots
            del total

            def two(i):
                b = info[at_listed + i]
                add_flows(b, r_out[i], info, lambda k: t_ref[i, k], local, nsucc, row, acc, nb)

            in_units(slots, two)
            sent[...] = acc[...].astype(BF16)

        def wrapped(*refs):
            refs = list(refs)
            scratch = refs.pop()
            scratch[...] = refs[5][...]
            refs[5] = scratch
            body(*refs)

        ins = [SMEM, VMEM, VMEM, VMEM, VMEM, VMEM, ANY, ANY] + ([] if first else [VMEM])
        return call(
            wrapped, ins,
            [
                (VMEM, (slots, s, d), BF16), (VMEM, (slots, s, d), BF16), (VMEM, (slots, s, d), F32),
            ],
            [
                pltpu.VMEM((rows, d), F32), pltpu.VMEM((slots, REMOTE, s, s), BF16),
                sems(1), sems(slots), pltpu.VMEM((slots, s, d), F32),
            ],
            16, slots * REMOTE * pair, 4 << 20, "join",
        )

    def add_returned(info, got, back):
        back[...] = jnp.zeros_like(back)
        for i in range(slots):
            j = info[at_owner + i]
            back[j] = back[j] + got[i].astype(F32)

    def close_body(info, got, totl, wl, back_in, vis_in, vis_out, back, stage, sem):
        del vis_in
        back[...] = back_in[...]
        for i in range(slots):
            j = info[at_owner + i]
            back[j] = back[j] + got[i].astype(F32)
        for i in range(slots):
            stage[i] = (wl[i].astype(F32) * (totl[i] + back[i])).astype(BF16)

        def cp(i):
            return pltpu.make_async_copy(stage.at[i], vis_out.at[info[at_listed + i]], sem.at[i])

        for i in range(slots):
            @pl.when(info[at_lead + i] == 1)
            def _(i=i):
                cp(i).start()

        for i in range(slots):
            @pl.when(info[at_lead + i] == 1)
            def _(i=i):
                cp(i).wait()

    close = pl.pallas_call(
        close_body,
        out_shape=sds((nb, s, d), BF16),
        in_specs=[SMEM] + [VMEM] * 4 + [ANY],
        out_specs=ANY,
        scratch_shapes=[
            pltpu.VMEM((slots, s, d), F32), pltpu.VMEM((slots, s, d), BF16), sems(slots),
        ],
        input_output_aliases={5: 0},
        compiler_params=pltpu.CompilerParams(vmem_limit_bytes=16 << 20),
        cost_estimate=pl.CostEstimate(flops=blk, bytes_accessed=2 << 20, transcendentals=0),
        name="close",
    )

    return dict(
        pack=pack, begin=begin, sweep_first=sweep_first, listed_next=listed_next,
        sweep_next=sweep_next, last=last, spread=make_spread, join=make_join, close=close,
    )


class WeightView:
    def __init__(self, ref, rows):
        self.ref, self.rows = ref, rows

    def __getitem__(self, e):
        return self.ref[e, 0 : self.rows]


def swap(parcels, axis):
    return lax.all_to_all(parcels, axis, split_axis=0, concat_axis=0, tiled=True)


def total_over(x, axis):
    n = lax.axis_size(axis)
    return jnp.sum(swap(jnp.broadcast_to(x[None], (n,) + x.shape), axis), axis=0)


def on_device(
    coarse, region_map, features, reward_weights, transitions, successors,
    part_sizes, outgoing_block_list, destinations, anchors,
):
    nb, nsucc, s, _ = transitions.shape
    rdev, d = coarse.shape
    n_dom = lax.axis_size("dom")
    per_peer = outgoing_block_list.shape[2]
    slots = n_dom * per_peer
    feat = features.shape[0]
    grp_first = lax.axis_index("grp") * n_dom
    linear = grp_first + lax.axis_index("dom")
    ks = make_kernels(nb, nsucc, s, d, slots, n_dom, rdev)

    listed = outgoing_block_list.reshape(slots)
    same = listed[:, None] == listed[None, :]
    owner = jnp.argmax(same, axis=1).astype(I32)
    lead = (owner == jnp.arange(slots, dtype=I32)).astype(I32)
    free = 1 - jnp.any(listed[None, :] == jnp.arange(nb, dtype=I32)[:, None], axis=1).astype(I32)
    base = linear * (nb * s)
    info = jnp.concatenate(
        [
            jnp.stack([base, grp_first, part_sizes[0], jnp.int32(0)]).astype(I32),
            successors.reshape(nb * nsucc), listed, lead, owner, free,
        ]
    )
    regions = region_map.reshape(nb, s)
    (parcels,) = ks["pack"](info, coarse, regions)
    rec = swap(parcels, "dom")

    rewards = jnp.dot(
        reward_weights[None, :], features.astype(F32), precision=lax.Precision.HIGHEST
    )[0]
    cst = jnp.concatenate(
        [
            jnp.pad(rewards.reshape(nb, s).T, ((0, 0), (0, 128 - nb))),
            jnp.broadcast_to((destinations - base).astype(F32)[None, :], (8, d)),
        ],
        axis=0,
    )

    w0, top0, sent = ks["begin"](info, rec, regions, cst, transitions)
    got = swap(sent, "dom")
    acc, peak, accl = ks["sweep_first"](info, cst, transitions, w0, top0)
    sent, wr = ks["listed_next"](info, got, accl, cst, transitions)
    got = swap(sent, "dom")
    w2, top2, acc, peak, wl = ks["sweep_next"](info, wr, cst, transitions, acc, peak)
    values, inv, r, row, sent, invl = ks["last"](
        info, got, cst, transitions, acc, peak, top2, anchors.reshape(nb, s, d)
    )
    got = swap(sent, "dom")
    total, r, ownl, part = ks["spread"](True, False)(info, row, transitions, r, w2, inv)
    sent, rl, back = ks["join"](True)(info, got, ownl, invl, wl, part, row, transitions)
    got = swap(sent, "dom")
    total, r, ownl, part = ks["spread"](False, False)(
        info, rl, row, transitions, r, w2, inv, total
    )
    sent, rl, back = ks["join"](False)(info, got, ownl, invl, wl, part, row, transitions, back)
    got = swap(sent, "dom")
    visits, totl = ks["spread"](False, True)(info, rl, row, transitions, r, w2, total)
    visits = ks["close"](info, got, totl, wl, back, visits)

    values = values.reshape(nb * s, d)
    visits = visits.reshape(nb * s, d)
    live_rows = (jnp.arange(nb * s, dtype=I32) // s < part_sizes[0])[:, None]
    mass = jnp.sum(jnp.where(live_rows, anchors.astype(F32), 0.0), axis=0, keepdims=True)
    part_counts = jnp.dot(features, visits, preferred_element_type=F32)
    sums = jnp.concatenate([part_counts, jnp.broadcast_to(mass, (8, d))], axis=0)
    sums = total_over(total_over(sums, "dom"), "grp")
    return values, visits, sums[:feat] / sums[feat : feat + 1]


def solution(mesh):
    every = ("grp", "dom")
    return jax.shard_map(
        on_device,
        mesh=mesh,
        in_specs=(
            P(every, None), P(every), P(None, every), P(), P(every, None, None, None),
            P(every, None), P(every), P(every, None, None), P(), P(every, None),
        ),
        out_specs=(P(every, None), P(every, None), P()),
        check_vma=False,
    )
```

profile of v0, /device:TPU:0, one launch (start us, length us, event | category | flops | bytes accessed | tf_op | source)
XLA Modules:
  0.0 203.2 jit_solution(14203795180023610478)
XLA Ops:
  0.6 1.4 iota_reduce_fusion
  5.8 0.8 copy-done.56
  6.7 1.3 pack.1
  7.9 7.3 %all-to-all-start = ((bf16[8,144,128]{2,1,0:T(8,128)(2,1)}), bf16[8,144,128]{2,1,0:T(8,128)(2,1)S(1)}, u32[]{:S(2)}, u32[]{:S(2)}) async-start(bf16[8,144,128]{2,1,0:T(8,128)(2,1)} %pack.1), calls=%async_computation | async-start | bytes 589824 | tf_op jit(solution)/shard_map/all_to_all | solution.py:721
  15.2 0.9 fusion
  16.9 7.9 %all-to-all-done.rec = bf16[8,144,128]{2,1,0:T(8,128)(2,1)S(1)} async-done(((bf16[8,144,128]{2,1,0:T(8,128)(2,1)}), bf16[8,144,128]{2,1,0:T(8,128)(2,1)S(1)}, u32[]{:S(2)}, u32[]{:S(2)}) %all-to-all-start) | async-done | bytes 294944 | tf_op jit(solution)/shard_map/all_to_all | solution.py:721
  24.8 3.4 %copy-done.1 = bf16[32,8,128,128]{3,2,1,0:T(8,128)(2,1)S(1)} copy-done((bf16[32,8,128,128]{3,2,1,0:T(8,128)(2,1)S(1)}, bf16[32,8,128,128]{3,2,1,0:T(8,128)(2,1)}, u32[]{:S(2)}) %copy-start.1) | copy-done | bytes 8388632
  28.9 7.9 %begin.1 = (bf16[40,128,128]{2,1,0:T(8,128)(2,1)S(1)}, f32[40,128]{1,0:T(8,128)S(1)}, bf16[8,128,128]{2,1,0:T(8,128)(2,1)}) custom-call(s32[316]{0:T(512)S(1)} %concatenate.9.info.refs_0_, bf16[8,144,128]{2,1,0:T(8,128)(2,1)S(1)} %all-to-all-done.rec, s32[32,128]{1,0:T(8,128)S(1)} %bitcast.31, f32[136,128]{1,0:T(8,128)S(1)} %select_maximum_fusion.cst_hbm, ...), custom_call_target="tpu_custom_call" | custom-call | flops 1610612736 | bytes 4194304 | tf_op jit(solution)/shard_map/begin/pallas_call | solution.py:770
  36.8 1.1 copy-done.23
  37.9 3.6 %all-to-all-start.1 = ((bf16[8,128,128]{2,1,0:T(8,128)(2,1)}), bf16[8,128,128]{2,1,0:T(8,128)(2,1)S(1)}, u32[]{:S(2)}, u32[]{:S(2)}) async-start(bf16[8,128,128]{2,1,0:T(8,128)(2,1)} %get-tuple-element.40), calls=%async_computation.1 | async-start | bytes 524288 | tf_op jit(solution)/shard_map/all_to_all | solution.py:721
  41.5 3.4 %copy-done.2 = bf16[32,8,128,128]{3,2,1,0:T(8,128)(2,1)S(1)} copy-done((bf16[32,8,128,128]{3,2,1,0:T(8,128)(2,1)S(1)}, bf16[32,8,128,128]{3,2,1,0:T(8,128)(2,1)}, u32[]{:S(2)}) %copy-start.2) | copy-done | bytes 8388632
  44.9 1.3 copy-done.24
  46.2 7.2 %sweep_first.1 = (f32[32,128,128]{2,1,0:T(8,128)S(1)}, f32[32,128]{1,0:T(8,128)S(1)}, f32[8,136,128]{2,1,0:T(8,128)S(1)}) custom-call(s32[316]{0:T(512)S(1)} %concatenate.9.info.refs_0_, f32[136,128]{1,0:T(8,128)S(1)} %select_maximum_fusion.cst_hbm, bf16[32,8,128,128]{3,2,1,0:T(8,128)(2,1)S(1)} %copy-done.2, bf16[40,128,128]{2,1,0:T(8,128)(2,1)S(1)} %copy-done.24, ...), custom_call_target="tpu_custom_call" | custom-call | flops 1744830464 | bytes 12582912 | tf_op jit(solution)/shard_map/sweep_first/pallas_call | solution.py:772
  53.5 3.4 %copy-done.3 = bf16[32,8,128,128]{3,2,1,0:T(8,128)(2,1)S(1)} copy-done((bf16[32,8,128,128]{3,2,1,0:T(8,128)(2,1)S(1)}, bf16[32,8,128,128]{3,2,1,0:T(8,128)(2,1)}, u32[]{:S(2)}) %copy-start.3) | copy-done | bytes 8388632
  56.8 3.1 %listed_next.1 = (bf16[8,128,128]{2,1,0:T(8,128)(2,1)}, bf16[8,144,128]{2,1,0:T(8,128)(2,1)S(1)}) custom-call(s32[316]{0:T(512)S(1)} %concatenate.9.info.refs_0_, bf16[8,128,128]{2,1,0:T(8,128)(2,1)S(1)} %all-to-all-done.1.got, f32[8,136,128]{2,1,0:T(8,128)S(1)} %get-tuple-element.43.accl, f32[136,128]{1,0:T(8,128)S(1)} %select_maximum_fusion.cst_hbm, ...), custom_call_target="tpu_custom_call" | custom-call | flops 100663296 | bytes 3145728 | tf_op jit(solution)/shard_map/listed_next/pallas_call | solution.py:773
  60.6 6.0 %all-to-all-start.2 = ((bf16[8,128,128]{2,1,0:T(8,128)(2,1)}), bf16[8,128,128]{2,1,0:T(8,128)(2,1)}, u32[]{:S(2)}, u32[]{:S(2)}) async-start(bf16[8,128,128]{2,1,0:T(8,128)(2,1)} %get-tuple-element.44), calls=%async_computation.2 | async-start | bytes 524288 | tf_op jit(solution)/shard_map/all_to_all | solution.py:721
  66.6 3.4 %copy-done.4 = bf16[32,8,128,128]{3,2,1,0:T(8,128)(2,1)S(1)} copy-done((bf16[32,8,128,128]{3,2,1,0:T(8,128)(2,1)S(1)}, bf16[32,8,128,128]{3,2,1,0:T(8,128)(2,1)}, u32[]{:S(2)}) %copy-start.4) | copy-done | bytes 8388632
  70.0 1.0 copy-done.46
  71.0 6.3 %sweep_next.1 = (bf16[32,128,128]{2,1,0:T(8,128)(2,1)S(1)}, f32[32,128]{1,0:T(8,128)S(1)}, f32[32,128,128]{2,1,0:T(8,128)S(1)}, f32[32,128]{1,0:T(8,128)S(1)}, bf16[8,128,128]{2,1,0:T(8,128)(2,1)S(1)}) custom-call(s32[316]{0:T(512)S(1)} %concatenate.9.info.refs_0_, bf16[8,144,128]{2,1,0:T(8,128)(2,1)S(1)} %copy-done.46, ...), custom_call_target="tpu_custom_call" | custom-call | flops 1073741824 | bytes 14680064 | tf_op jit(solution)/shard_map/sweep_next/pallas_call | solution.py:775
  78.0 1.3 copy-done.18
  79.9 1.2 copy-done.8
  81.2 1.6 copy-done.19
  83.5 6.9 %last.1 = (bf16[32,128,128]{2,1,0:T(8,128)(2,1)}, f32[32,128,128]{2,1,0:T(8,128)S(1)}, bf16[32,128,128]{2,1,0:T(8,128)(2,1)S(1)}, f32[72,128]{1,0:T(8,128)S(1)},...) custom-call(s32[316]{0:T(512)S(1)} %concatenate.9.info.refs_0_, bf16[8,128,128]{2,1,0:T(8,128)(2,1)} %all-to-all-done.2.got, ...), custom_call_target="tpu_custom_call" | custom-call | flops 805306368 | bytes 14680064 | tf_op jit(solution)/shard_map/last/pallas_call | solution.py:776
  91.1 1.0 copy-done.29
  92.8 6.0 %all-to-all-start.3 = ((bf16[8,128,128]{2,1,0:T(8,128)(2,1)}), bf16[8,128,128]{2,1,0:T(8,128)(2,1)}, u32[]{:S(2)}, u32[]{:S(2)}) async-start(bf16[8,128,128]{2,1,0:T(8,128)(2,1)} %copy-done.52), calls=%async_computation.3 | async-start | bytes 524288 | tf_op jit(solution)/shard_map/all_to_all | solution.py:721
  98.8 1.2 copy-done.30
  100.0 6.9 %spread.3 = (f32[32,128,128]{2,1,0:T(8,128)S(1)}, bf16[32,128,128]{2,1,0:T(8,128)(2,1)S(1)}, f32[8,128,128]{2,1,0:T(8,128)S(1)}, f32[8,128,128]{2,1,0:T(8,128)S(1)}) custom-call(s32[316]{0:T(512)S(1)} %concatenate.9.info.refs_0_, f32[72,128]{1,0:T(8,128)S(1)} %get-tuple-element.53.refs_1_.refs_6_.refs_2_, bf16[32,8,128,128]{3,2,1,0:T(8,128)(2,1)} %refs_3_.3, ...), custom_call_target="tpu_custom_call" | custom-call | flops 1073741824 | bytes 14680064 | tf_op jit(solution)/shard_map/spread/pallas_call | solution.py:780
  107.0 1.3 copy-done.16
  108.3 1.0 copy-done.27
  109.3 0.8 copy-done.41
  110.9 3.4 %copy-done.5 = bf16[32,8,128,128]{3,2,1,0:T(8,128)(2,1)S(1)} copy-done((bf16[32,8,128,128]{3,2,1,0:T(8,128)(2,1)S(1)}, bf16[32,8,128,128]{3,2,1,0:T(8,128)(2,1)}, u32[]{:S(2)}) %copy-start.5) | copy-done | bytes 8388632
  114.3 0.9 copy-done.11
  115.2 1.0 copy-done.21
  116.3 1.0 copy-done.42
  117.3 1.0 copy-done.44
  118.4 2.8 %join.2 = (bf16[8,128,128]{2,1,0:T(8,128)(2,1)S(1)}, bf16[8,128,128]{2,1,0:T(8,128)(2,1)S(1)}, f32[8,128,128]{2,1,0:T(8,128)S(1)}) custom-call(s32[316]{0:T(512)S(1)} %concatenate.9.info.refs_0_, bf16[8,128,128]{2,1,0:T(8,128)(2,1)} %all-to-all-done.3.refs_1_, f32[8,128,128]{2,1,0:T(8,128)S(1)} %copy-done.42, f32[8,128,128]{2,1,0:T(8,128)S(1)} %copy-done.21, ...), custom_call_target="tpu_custom_call" | custom-call | flops 100663296 | bytes 4194304 | tf_op jit(solution)/shard_map/join/pallas_call | solution.py:781
  121.2 0.8 copy-done.33
  123.3 6.0 %all-to-all-start.4 = ((bf16[8,128,128]{2,1,0:T(8,128)(2,1)}), bf16[8,128,128]{2,1,0:T(8,128)(2,1)}, u32[]{:S(2)}, u32[]{:S(2)}) async-start(bf16[8,128,128]{2,1,0:T(8,128)(2,1)} %copy-done.53), calls=%async_computation.4 | async-start | bytes 524288 | tf_op jit(solution)/shard_map/all_to_all | solution.py:721
  129.3 1.6 copy-done.17
  130.9 1.2 copy-done.28
  132.2 0.9 copy-done.48
  133.1 7.1 %spread.4 = (f32[32,128,128]{2,1,0:T(8,128)S(1)}, bf16[32,128,128]{2,1,0:T(8,128)(2,1)S(1)}, f32[8,128,128]{2,1,0:T(8,128)S(1)}, f32[8,128,128]{2,1,0:T(8,128)S(1)}) custom-call(s32[316]{0:T(512)S(1)} %concatenate.9.info.refs_0_, bf16[8,128,128]{2,1,0:T(8,128)(2,1)S(1)} %copy-done.48, f32[72,128]{1,0:T(8,128)S(1)} %get-tuple-element.53.refs_1_.refs_6_.refs_2_, ...), custom_call_target="tpu_custom_call" | custom-call | flops 1073741824 | bytes 14680064 | tf_op jit(solution)/shard_map/spread/pallas_call | solution.py:783
  140.2 1.3 copy-done.14
  141.5 1.0 copy-done.25
  143.3 0.8 copy-done.37
  144.1 3.4 %copy-done.6 = bf16[32,8,128,128]{3,2,1,0:T(8,128)(2,1)S(1)} copy-done((bf16[32,8,128,128]{3,2,1,0:T(8,128)(2,1)S(1)}, bf16[32,8,128,128]{3,2,1,0:T(8,128)(2,1)}, u32[]{:S(2)}) %copy-start.6) | copy-done | bytes 8388632
  147.5 0.9 copy-done.12
  148.4 1.0 copy-done.22
  149.5 1.0 copy-done.34
  150.5 1.0 copy-done.36
  151.5 1.0 copy-done.38
  152.6 2.9 %join.3 = (bf16[8,128,128]{2,1,0:T(8,128)(2,1)S(1)}, bf16[8,128,128]{2,1,0:T(8,128)(2,1)S(1)}, f32[8,128,128]{2,1,0:T(8,128)S(1)}) custom-call(s32[316]{0:T(512)S(1)} %concatenate.9.info.refs_0_, bf16[8,128,128]{2,1,0:T(8,128)(2,1)} %all-to-all-done.4.refs_1_, f32[8,128,128]{2,1,0:T(8,128)S(1)} %copy-done.36, f32[8,128,128]{2,1,0:T(8,128)S(1)} %copy-done.22, ...), custom_call_target="tpu_custom_call" | custom-call | flops 100663296 | bytes 4194304 | tf_op jit(solution)/shard_map/join/pallas_call | solution.py:786
  157.7 6.1 %all-to-all-start.5 = ((bf16[8,128,128]{2,1,0:T(8,128)(2,1)}), bf16[8,128,128]{2,1,0:T(8,128)(2,1)}, u32[]{:S(2)}, u32[]{:S(2)}) async-start(bf16[8,128,128]{2,1,0:T(8,128)(2,1)} %copy-done.51), calls=%async_computation.5 | async-start | bytes 524288 | tf_op jit(solution)/shard_map/all_to_all | solution.py:721
  163.9 2.2 %select_reduce_fusion = f32[128]{0:T(128)S(1)} fusion(bf16[4096,128]{1,0:T(8,128)(2,1)S(1)} %copy-done.9, pred[4096]{0:T(1024)(128)(4,1)S(1)} %fusion.3), kind=kLoop, calls=%fused_computation | loop fusion | flops 1572736 | bytes 1053184 | tf_op jit(solution)/shard_map/reduce_sum | solution.py:794
  166.0 3.4 %copy-done.7 = bf16[32,8,128,128]{3,2,1,0:T(8,128)(2,1)S(1)} copy-done((bf16[32,8,128,128]{3,2,1,0:T(8,128)(2,1)S(1)}, bf16[32,8,128,128]{3,2,1,0:T(8,128)(2,1)}, u32[]{:S(2)}) %copy-start.7) | copy-done | bytes 8388632
  169.4 1.6 copy-done.15
  171.0 0.9 copy-done.50
  171.9 5.0 %spread.5 = (bf16[32,128,128]{2,1,0:T(8,128)(2,1)}, f32[8,128,128]{2,1,0:T(8,128)S(1)}) custom-call(s32[316]{0:T(512)S(1)} %concatenate.9.info.refs_0_, bf16[8,128,128]{2,1,0:T(8,128)(2,1)S(1)} %copy-done.50, f32[72,128]{1,0:T(8,128)S(1)} %get-tuple-element.53.refs_1_.refs_6_.refs_2_, bf16[32,8,128,128]{3,2,1,0:T(8,128)(2,1)S(1)} %copy-done.7, ...), custom_call_target="tpu_custom_call" | custom-call | flops 671088640 | bytes 14680064 | tf_op jit(solution)/shard_map/spread/pallas_call | solution.py:788
  177.0 0.8 copy-done.39
  177.8 1.0 copy-done.40
  178.8 1.9 close.1
  180.7 1.5 convolution_bitcast_fusion
  182.3 13.4 %all_to_all.40 = f32[8,40,128]{2,1,0:T(8,128)S(1)} all-to-all(f32[8,40,128]{2,1,0:T(8,128)S(1)} %broadcast_in_dim.24), channel_id=1, replica_groups=mesh['grp'=4,'dom'=8] {'dom'}, dimensions={0} | all-to-all | bytes 327680 | tf_op jit(solution)/shard_map/all_to_all | solution.py:721
  195.7 6.8 %all_to_all.41 = f32[4,40,128]{2,1,0:T(8,128)S(1)} all-to-all(f32[4,40,128]{2,1,0:T(8,128)S(1)} %broadcast_in_dim.25), channel_id=1, replica_groups=mesh['grp'=4,'dom'=8] {'grp'}, dimensions={0} | all-to-all | bytes 163840 | tf_op jit(solution)/shard_map/all_to_all | solution.py:721
  (103 shorter events, 14.7 us)
Async XLA Ops:
  0.6 14.6 %copy-start = (bf16[32,4096]{1,0:T(8,128)(2,1)S(1)}, bf16[32,4096]{1,0:T(8,128)(2,1)}, u32[]{:S(2)}) copy-start(bf16[32,4096]{1,0:T(8,128)(2,1)} %param.12) | copy-start | bytes 786436
  5.1 0.7 copy-start.54
  5.8 0.8 copy-start.56
  7.9 16.9 %all-to-all-start = ((bf16[8,144,128]{2,1,0:T(8,128)(2,1)}), bf16[8,144,128]{2,1,0:T(8,128)(2,1)S(1)}, u32[]{:S(2)}, u32[]{:S(2)}) async-start(bf16[8,144,128]{2,1,0:T(8,128)(2,1)} %pack.1), calls=%async_computation | async-start | bytes 589824 | tf_op jit(solution)/shard_map/all_to_all | solution.py:721
  24.8 3.4 %copy-start.1 = (bf16[32,8,128,128]{3,2,1,0:T(8,128)(2,1)S(1)}, bf16[32,8,128,128]{3,2,1,0:T(8,128)(2,1)}, u32[]{:S(2)}) copy-start(bf16[32,8,128,128]{3,2,1,0:T(8,128)(2,1)} %refs_3_.3) | copy-start | bytes 25165828
  28.2 0.7 copy-start.55
  36.8 1.1 copy-start.23
  37.9 15.5 %all-to-all-start.1 = ((bf16[8,128,128]{2,1,0:T(8,128)(2,1)}), bf16[8,128,128]{2,1,0:T(8,128)(2,1)S(1)}, u32[]{:S(2)}, u32[]{:S(2)}) async-start(bf16[8,128,128]{2,1,0:T(8,128)(2,1)} %get-tuple-element.40), calls=%async_computation.1 | async-start | bytes 524288 | tf_op jit(solution)/shard_map/all_to_all | solution.py:721
  41.5 3.4 %copy-start.2 = (bf16[32,8,128,128]{3,2,1,0:T(8,128)(2,1)S(1)}, bf16[32,8,128,128]{3,2,1,0:T(8,128)(2,1)}, u32[]{:S(2)}) copy-start(bf16[32,8,128,128]{3,2,1,0:T(8,128)(2,1)} %refs_3_.3) | copy-start | bytes 25165828
  44.9 1.3 copy-start.24
  53.4 3.4 %copy-start.3 = (bf16[32,8,128,128]{3,2,1,0:T(8,128)(2,1)S(1)}, bf16[32,8,128,128]{3,2,1,0:T(8,128)(2,1)}, u32[]{:S(2)}) copy-start(bf16[32,8,128,128]{3,2,1,0:T(8,128)(2,1)} %refs_3_.3) | copy-start | bytes 25165828
  59.9 0.7 copy-start.45
  60.6 19.3 %all-to-all-start.2 = ((bf16[8,128,128]{2,1,0:T(8,128)(2,1)}), bf16[8,128,128]{2,1,0:T(8,128)(2,1)}, u32[]{:S(2)}, u32[]{:S(2)}) async-start(bf16[8,128,128]{2,1,0:T(8,128)(2,1)} %get-tuple-element.44), calls=%async_computation.2 | async-start | bytes 524288 | tf_op jit(solution)/shard_map/all_to_all | solution.py:721
  66.6 3.4 %copy-start.4 = (bf16[32,8,128,128]{3,2,1,0:T(8,128)(2,1)S(1)}, bf16[32,8,128,128]{3,2,1,0:T(8,128)(2,1)}, u32[]{:S(2)}) copy-start(bf16[32,8,128,128]{3,2,1,0:T(8,128)(2,1)} %refs_3_.3) | copy-start | bytes 25165828
  70.0 1.0 copy-start.46
  77.3 0.7 copy-start.10
  78.0 1.3 copy-start.18
  79.9 1.2 copy-start.8
  81.2 1.6 copy-start.19
  82.7 0.7 copy-start.58
  90.3 0.8 copy-start.20
  91.1 1.0 copy-start.29
  92.1 0.7 copy-start.52
  92.8 18.1 %all-to-all-start.3 = ((bf16[8,128,128]{2,1,0:T(8,128)(2,1)}), bf16[8,128,128]{2,1,0:T(8,128)(2,1)}, u32[]{:S(2)}, u32[]{:S(2)}) async-start(bf16[8,128,128]{2,1,0:T(8,128)(2,1)} %copy-done.52), calls=%async_computation.3 | async-start | bytes 524288 | tf_op jit(solution)/shard_map/all_to_all | solution.py:721
  98.8 1.2 copy-start.30
  107.0 1.3 copy-start.16
  108.3 1.0 copy-start.27
  109.3 0.8 copy-start.41
  110.1 0.8 copy-start.43
  110.9 3.4 %copy-start.5 = (bf16[32,8,128,128]{3,2,1,0:T(8,128)(2,1)S(1)}, bf16[32,8,128,128]{3,2,1,0:T(8,128)(2,1)}, u32[]{:S(2)}) copy-start(bf16[32,8,128,128]{3,2,1,0:T(8,128)(2,1)} %refs_3_.3) | copy-start | bytes 25165828
  114.3 0.9 copy-start.11
  115.2 1.0 copy-start.21
  116.3 1.0 copy-start.42
  117.3 1.0 copy-start.44
  121.1 0.8 copy-start.33
  121.9 0.7 copy-start.47
  122.6 0.7 copy-start.53
  123.3 20.7 %all-to-all-start.4 = ((bf16[8,128,128]{2,1,0:T(8,128)(2,1)}), bf16[8,128,128]{2,1,0:T(8,128)(2,1)}, u32[]{:S(2)}, u32[]{:S(2)}) async-start(bf16[8,128,128]{2,1,0:T(8,128)(2,1)} %copy-done.53), calls=%async_computation.4 | async-start | bytes 524288 | tf_op jit(solution)/shard_map/all_to_all | solution.py:721
  129.3 1.6 copy-start.17
  130.9 1.2 copy-start.28
  132.2 0.9 copy-start.48
  140.2 1.3 copy-start.14
  141.5 1.0 copy-start.25
  142.5 0.8 copy-start.35
  143.3 0.8 copy-start.37
  144.1 3.4 %copy-start.6 = (bf16[32,8,128,128]{3,2,1,0:T(8,128)(2,1)S(1)}, bf16[32,8,128,128]{3,2,1,0:T(8,128)(2,1)}, u32[]{:S(2)}) copy-start(bf16[32,8,128,128]{3,2,1,0:T(8,128)(2,1)} %refs_3_.3) | copy-start | bytes 25165828
  147.5 0.9 copy-start.12
  148.4 1.0 copy-start.22
  149.5 1.0 copy-start.34
  150.5 1.0 copy-start.36
  151.5 1.0 copy-start.38
  152.6 11.3 %copy-start.9 = (bf16[4096,128]{1,0:T(8,128)(2,1)S(1)}, bf16[4096,128]{1,0:T(8,128)(2,1)}, u32[]{:S(2)}) copy-start(bf16[4096,128]{1,0:T(8,128)(2,1)} %param.19) | copy-start | bytes 3145732
  155.5 0.8 copy-start.31
  156.3 0.7 copy-start.49
  157.0 0.7 copy-start.51
  157.7 8.3 %copy-start.26 = (bf16[32,128,128]{2,1,0:T(8,128)(2,1)S(1)}, bf16[32,128,128]{2,1,0:T(8,128)(2,1)}, u32[]{:S(2)}) copy-start(bf16[32,128,128]{2,1,0:T(8,128)(2,1)} %copy-done.25) | copy-start | bytes 3145732
  157.7 20.1 %all-to-all-start.5 = ((bf16[8,128,128]{2,1,0:T(8,128)(2,1)}), bf16[8,128,128]{2,1,0:T(8,128)(2,1)}, u32[]{:S(2)}, u32[]{:S(2)}) async-start(bf16[8,128,128]{2,1,0:T(8,128)(2,1)} %copy-done.51), calls=%async_computation.5 | async-start | bytes 524288 | tf_op jit(solution)/shard_map/all_to_all | solution.py:721
  166.0 3.4 %copy-start.7 = (bf16[32,8,128,128]{3,2,1,0:T(8,128)(2,1)S(1)}, bf16[32,8,128,128]{3,2,1,0:T(8,128)(2,1)}, u32[]{:S(2)}) copy-start(bf16[32,8,128,128]{3,2,1,0:T(8,128)(2,1)} %refs_3_.3) | copy-start | bytes 25165828
  169.4 1.6 copy-start.15
  171.0 0.9 copy-start.50
  171.9 5.9 %copy-start.13 = (bf16[8,128,128]{2,1,0:T(8,128)(2,1)S(1)}, bf16[8,128,128]{2,1,0:T(8,128)(2,1)}, u32[]{:S(2)}) copy-start(bf16[8,128,128]{2,1,0:T(8,128)(2,1)} %copy-done.10) | copy-start | bytes 786436
  171.9 5.9 %copy-start.32 = (f32[8,128,128]{2,1,0:T(8,128)S(1)}, f32[8,128,128]{2,1,0:T(8,128)}, u32[]{:S(2)}) copy-start(f32[8,128,128]{2,1,0:T(8,128)} %copy-done.31) | copy-start | bytes 1572868
  177.0 0.8 copy-start.39
  177.8 1.0 copy-start.40
  (1 other events, 0.6 us)
where the time goes:
time: 206 us; the launch traced here: 203 us
  local copies, waits for them, and re-layouts  71.1 us (35%)
  Pallas kernels  59.2 us (29%)
  starting transfers between devices  35 us (17%)
  blocking collectives  20.2 us (10%)
  waiting for transfers between devices  7.96 us (4%)
  other arithmetic  5.65 us (3%)
  matrix products  2.38 us (1%)
    unnamed x119, local copies, waits for them, and re-layouts  70.1 us
    all_to_all x6, starting transfers between devices, swap(): lax.all_to_all(parcels, axis, split_axis=0, concat_axis=0, tiled=True)  35 us
    all_to_all x2, blocking collectives, swap(): lax.all_to_all(parcels, axis, split_axis=0, concat_axis=0, tiled=True)  20.2 us
    all_to_all x6, waiting for transfers between devices, swap(): lax.all_to_all(parcels, axis, split_axis=0, concat_axis=0, tiled=True)  7.96 us
    pallas_call x1, Pallas kernels, on_device(): w0, top0, sent = ks['begin'](info, rec, regions, cst, transitions)  7.87 us
    pallas_call x1, Pallas kernels, on_device(): acc, peak, accl = ks['sweep_first'](info, cst, transitions, w0, top0)  7.18 us
    pallas_call x1, Pallas kernels, on_device(): ks['spread'](False, False)(info, rl, row, transitions, r, w2, inv, total)  7.07 us
    pallas_call x1, Pallas kernels, on_device(): ks['spread'](True, False)(info, row, transitions, r, w2, inv)  6.95 us
  transfers between devices with their start and end apart: 6, of which 1 were waited for; matrix products, arithmetic and copies ran while one was open for 2% of the time, Pallas kernels for 16%

commit v1 on v0

--- a/solution.py
+++ b/solution.py
@@ -10,6 +10,7 @@
 REMOTE = 3
 EXTRA = 16
 UNIT = 8
+GRANT = 60 * 1024 * 1024
 ANY = pl.BlockSpec(memory_space=pltpu.HBM)
 VMEM = pl.BlockSpec(memory_space=pltpu.VMEM)
 SMEM = pl.BlockSpec(memory_space=pltpu.SMEM)
@@ -30,14 +31,14 @@
     return lax.dot_general(a, b, (((0,), (0,)), ((), ())), preferred_element_type=F32)
 
 
-def call(body, ins, outs, scratch, mib, flops, nbytes, name):
+def call(body, ins, outs, scratch, flops, nbytes, name):
     return pl.pallas_call(
         body,
         out_shape=tuple(sds(shape, dtype) for _, shape, dtype in outs),
         in_specs=list(ins),
         out_specs=tuple(space for space, _, _ in outs),
         scratch_shapes=scratch,
-        compiler_params=pltpu.CompilerParams(vmem_limit_bytes=mib << 20),
+        compiler_params=pltpu.CompilerParams(vmem_limit_bytes=GRANT),
         cost_estimate=pl.CostEstimate(flops=flops, bytes_accessed=nbytes, transcendentals=0),
         name=name,
     )
@@ -165,7 +166,7 @@
     pack = call(
         pack_body, [SMEM, VMEM, VMEM],
         [(VMEM, (n_dom, rdev + per_peer * EXTRA, d), BF16)],
-        [], 8, blk, 1 << 20, "pack",
+        [], blk, 1 << 20, "pack",
     )
 
     def begin_body(
@@ -260,7 +261,7 @@
             pltpu.VMEM((s, 128), F32), pltpu.VMEM((nl, d), F32), const_spec(),
             pltpu.VMEM((slots, nsucc, s, s), BF16), sems(3), sems(slots),
         ],
-        32, 2 * nl * s * n_dom * rdev * d + slots * nsucc * pair, 4 << 20, "begin",
+        2 * nl * s * n_dom * rdev * d + slots * nsucc * pair, 4 << 20, "begin",
     )
 
     def finish_local(info, t_ref, w_ref, top_ref, acc, peak, accl, acc_out, peak_out, put, sem, n0):
@@ -316,7 +317,7 @@
             pltpu.VMEM((nb, s, d), F32), pltpu.VMEM((nb, d), F32),
             sems(4), pltpu.SemaphoreType.DMA((2, turns)),
         ],
-        40, nb * (nsucc + local) * pair, 12 << 20, "sweep_first",
+        nb * (nsucc + local) * pair, 12 << 20, "sweep_first",
     )
 
     def listed_next_body(info, got, accl, cst_hbm, t_hbm, sent, wr_out, cst, t_ref, topr, sem, t_sem):
@@ -356,7 +357,7 @@
             const_spec(), pltpu.VMEM((slots, REMOTE, s, s), BF16), pltpu.VMEM((slots, d), F32),
             sems(1), sems(slots),
         ],
-        16, slots * REMOTE * pair, 3 << 20, "listed_next",
+        slots * REMOTE * pair, 3 << 20, "listed_next",
     )
 
     def sweep_next_body(
@@ -409,7 +410,7 @@
             pltpu.VMEM((slots, s + 8, d), F32),
             sems(4), pltpu.SemaphoreType.DMA((4, turns)),
         ],
-        40, nb * nsucc * pair, 14 << 20, "sweep_next",
+        nb * nsucc * pair, 14 << 20, "sweep_next",
     )
 
     def add_flows(b, r, info, t_of, k0, k1, row, acc, base):
@@ -487,7 +488,7 @@
             pltpu.VMEM((slots, s, d), F32),
             sems(4), pltpu.SemaphoreType.DMA((6, turns)),
         ],
-        40, nb * 2 * REMOTE * pair, 14 << 20, "last",
+        nb * 2 * REMOTE * pair, 14 << 20, "last",
     )
 
     def make_spread(first, final):
@@ -596,7 +597,7 @@
             scratch.append(pltpu.VMEM((nb, s, d), BF16))
         else:
             scratch += [pltpu.VMEM((nb, s, d), F32), pltpu.VMEM((nb, s, d), BF16)]
-        return call(body, ins, outs, scratch, 40, nb * ks * pair, 14 << 20, "spread")
+        return call(body, ins, outs, scratch, nb * ks * pair, 14 << 20, "spread")
 
     def make_join(first):
         def body(*refs):
@@ -658,7 +659,7 @@
                 pltpu.VMEM((rows, d), F32), pltpu.VMEM((slots, REMOTE, s, s), BF16),
                 sems(1), sems(slots), pltpu.VMEM((slots, s, d), F32),
             ],
-            16, slots * REMOTE * pair, 4 << 20, "join",
+            slots * REMOTE * pair, 4 << 20, "join",
         )
 
     def add_returned(info, got, back):
@@ -698,7 +699,7 @@
             pltpu.VMEM((slots, s, d), F32), pltpu.VMEM((slots, s, d), BF16), sems(slots),
         ],
         input_output_aliases={5: 0},
-        compiler_params=pltpu.CompilerParams(vmem_limit_bytes=16 << 20),
+        compiler_params=pltpu.CompilerParams(vmem_limit_bytes=GRANT),
         cost_estimate=pl.CostEstimate(flops=blk, bytes_accessed=2 << 20, transcendentals=0),
         name="close",
     )

time: 206 us -> 170 us (0.83)
  local copies, waits for them, and re-layouts: 71.1 us -> 6.51 us
  Pallas kernels: 59.2 us -> 89.1 us
    unnamed x119 -> x17, local copies, waits for them, and re-layouts: 70.1 us -> 4.96 us
    pallas_call x1, Pallas kernels: 7.07 us -> 12.2 us  [on_device(): ks['spread'](False, False)(info, rl, row, transitions, r, w2, inv, total)]
    pallas_call x1, Pallas kernels: 6.3 us -> 10.9 us  [on_device(): ks['sweep_next'](info, wr, cst, transitions, acc, peak)]
    pallas_call x1, Pallas kernels: 6.95 us -> 11.3 us  [on_device(): ks['spread'](True, False)(info, row, transitions, r, w2, inv)]
    pallas_call x1, Pallas kernels: 7.18 us -> 11.1 us  [on_device(): acc, peak, accl = ks['sweep_first'](info, cst, transitions, w0, top0)]
    pallas_call x1, Pallas kernels: 5.03 us -> 8.73 us  [on_device(): ks['spread'](False, True)(info, rl, row, transitions, r, w2, total)]
    pallas_call x1, Pallas kernels: 6.87 us -> 8.97 us  [on_device(): ks['last']]
  transfers between devices with their start and end apart: 6 -> 6, of which waited for: 1 -> 1; matrix products, arithmetic and copies ran while one was open for 2% -> 3% of each run, Pallas kernels for 16% -> 32%
where the time goes in v1:
time: 170 us; the launch traced here: 168 us
  Pallas kernels  89.1 us (52%)
  starting transfers between devices  35 us (21%)
  blocking collectives  20.2 us (12%)
  waiting for transfers between devices  7.34 us (4%)
  local copies, waits for them, and re-layouts  6.51 us (4%)
  other arithmetic  6.27 us (4%)
  matrix products  2.38 us (1%)
    all_to_all x6, starting transfers between devices, swap(): lax.all_to_all(parcels, axis, split_axis=0, concat_axis=0, tiled=True)  35 us
    all_to_all x2, blocking collectives, swap(): lax.all_to_all(parcels, axis, split_axis=0, concat_axis=0, tiled=True)  20.2 us
    pallas_call x1, Pallas kernels, on_device(): ks['spread'](False, False)(info, rl, row, transitions, r, w2, inv, total)  12.2 us
    pallas_call x1, Pallas kernels, on_device(): ks['spread'](True, False)(info, row, transitions, r, w2, inv)  11.3 us
    pallas_call x1, Pallas kernels, on_device(): acc, peak, accl = ks['sweep_first'](info, cst, transitions, w0, top0)  11.1 us
    pallas_call x1, Pallas kernels, on_device(): ks['sweep_next'](info, wr, cst, transitions, acc, peak)  10.9 us
    pallas_call x1, Pallas kernels, on_device(): w0, top0, sent = ks['begin'](info, rec, regions, cst, transitions)  9.58 us
    pallas_call x1, Pallas kernels, on_device(): ks['last']  8.97 us
  transfers between devices with their start and end apart: 6, of which 1 were waited for; matrix products, arithmetic and copies ran while one was open for 3% of the time, Pallas kernels for 32%

profile of v1, /device:TPU:0, one launch (start us, length us, event | category | flops | bytes accessed | tf_op | source)
XLA Modules:
  0.0 168.3 jit_solution(17484668358441503983)
XLA Ops:
  0.6 0.0 copy-start
  0.6 1.4 iota_reduce_fusion
  2.1 0.7 fusion.7
  3.5 0.8 copy.15
  4.2 0.1 reshape.49
  4.4 1.3 concatenate.9.info.refs_0_
  5.7 1.6 pack.1
  7.3 7.3 %all-to-all-start = ((bf16[8,144,128]{2,1,0:T(8,128)(2,1)}), bf16[8,144,128]{2,1,0:T(8,128)(2,1)S(1)}, u32[]{:S(2)}, u32[]{:S(2)}) async-start(bf16[8,144,128]{2,1,0:T(8,128)(2,1)} %pack.1), calls=%async_computation | async-start | bytes 589824 | tf_op jit(solution)/shard_map/all_to_all | solution.py:722
  14.6 0.0 copy-done
  14.6 0.9 fusion
  15.4 0.1 copy.17
  15.5 0.7 subtract_convert_fusion
  16.2 0.6 select_maximum_fusion.cst_hbm
  16.9 7.3 %all-to-all-done.rec = bf16[8,144,128]{2,1,0:T(8,128)(2,1)S(1)} async-done(((bf16[8,144,128]{2,1,0:T(8,128)(2,1)}), bf16[8,144,128]{2,1,0:T(8,128)(2,1)S(1)}, u32[]{:S(2)}, u32[]{:S(2)}) %all-to-all-start) | async-done | bytes 294944 | tf_op jit(solution)/shard_map/all_to_all | solution.py:722
  24.2 0.0 copy-start.2
  24.2 0.7 copy-done.2
  24.9 9.6 %begin.1 = (bf16[40,128,128]{2,1,0:T(8,128)(2,1)}, f32[40,128]{1,0:T(8,128)}, bf16[8,128,128]{2,1,0:T(8,128)(2,1)}) custom-call(s32[316]{0:T(512)} %concatenate.9.info.refs_0_, bf16[8,144,128]{2,1,0:T(8,128)(2,1)} %copy-done.2, s32[32,128]{1,0:T(8,128)} %bitcast.34, f32[136,128]{1,0:T(8,128)} %select_maximum_fusion.cst_hbm, bf16[32,8,128,128]{3,2,1,0:T(8,128)(2,1)} %refs_3_.3), custom_call_target="tpu_custom_call" | custom-call | flops 1610612736 | bytes 4194304 | tf_op jit(solution)/shard_map/begin/pallas_call | solution.py:771
  34.5 3.6 %all-to-all-start.1 = ((bf16[8,128,128]{2,1,0:T(8,128)(2,1)}), bf16[8,128,128]{2,1,0:T(8,128)(2,1)S(1)}, u32[]{:S(2)}, u32[]{:S(2)}) async-start(bf16[8,128,128]{2,1,0:T(8,128)(2,1)} %get-tuple-element.40), calls=%async_computation.1 | async-start | bytes 524288 | tf_op jit(solution)/shard_map/all_to_all | solution.py:722
  38.1 11.1 %sweep_first.1 = (f32[32,128,128]{2,1,0:T(8,128)}, f32[32,128]{1,0:T(8,128)}, f32[8,136,128]{2,1,0:T(8,128)}) custom-call(s32[316]{0:T(512)} %concatenate.9.info.refs_0_, f32[136,128]{1,0:T(8,128)} %select_maximum_fusion.cst_hbm, bf16[32,8,128,128]{3,2,1,0:T(8,128)(2,1)} %refs_3_.3, bf16[40,128,128]{2,1,0:T(8,128)(2,1)} %get-tuple-element.41.w_hbm, ...), custom_call_target="tpu_custom_call" | custom-call | flops 1744830464 | bytes 12582912 | tf_op jit(solution)/shard_map/sweep_first/pallas_call | solution.py:773
  49.2 0.0 all-to-all-done.1.got
  49.2 0.0 copy-start.7
  49.2 0.7 copy-done.7
  49.9 3.6 %listed_next.1 = (bf16[8,128,128]{2,1,0:T(8,128)(2,1)}, bf16[8,144,128]{2,1,0:T(8,128)(2,1)}) custom-call(s32[316]{0:T(512)} %concatenate.9.info.refs_0_, bf16[8,128,128]{2,1,0:T(8,128)(2,1)} %copy-done.7, f32[8,136,128]{2,1,0:T(8,128)} %get-tuple-element.43.accl, f32[136,128]{1,0:T(8,128)} %select_maximum_fusion.cst_hbm, bf16[32,8,128,128]{3,2,1,0:T(8,128)(2,1)} %refs_3_.3), custom_call_target="tpu_custom_call" | custom-call | flops 100663296 | bytes 3145728 | tf_op jit(solution)/shard_map/listed_next/pallas_call | solution.py:774
  53.5 6.0 %all-to-all-start.2 = ((bf16[8,128,128]{2,1,0:T(8,128)(2,1)}), bf16[8,128,128]{2,1,0:T(8,128)(2,1)S(1)}, u32[]{:S(2)}, u32[]{:S(2)}) async-start(bf16[8,128,128]{2,1,0:T(8,128)(2,1)} %get-tuple-element.44), calls=%async_computation.2 | async-start | bytes 524288 | tf_op jit(solution)/shard_map/all_to_all | solution.py:722
  59.6 10.9 %sweep_next.1 = (bf16[32,128,128]{2,1,0:T(8,128)(2,1)}, f32[32,128]{1,0:T(8,128)}, f32[32,128,128]{2,1,0:T(8,128)}, f32[32,128]{1,0:T(8,128)}, bf16[8,128,128]{2,1,0:T(8,128)(2,1)}) custom-call(s32[316]{0:T(512)} %concatenate.9.info.refs_0_, bf16[8,144,128]{2,1,0:T(8,128)(2,1)} %get-tuple-element.45.wr, f32[136,128]{1,0:T(8,128)} %select_maximum_fusion.cst_hbm, ...), custom_call_target="tpu_custom_call" | custom-call | flops 1073741824 | bytes 14680064 | tf_op jit(solution)/shard_map/sweep_next/pallas_call | solution.py:776
  70.5 0.0 all-to-all-done.2.got
  70.5 0.0 copy-start.3
  70.5 0.7 copy-done.3
  71.2 9.0 %last.1 = (bf16[32,128,128]{2,1,0:T(8,128)(2,1)}, f32[32,128,128]{2,1,0:T(8,128)}, bf16[32,128,128]{2,1,0:T(8,128)(2,1)}, f32[72,128]{1,0:T(8,128)}, bf16[8,128,...) custom-call(s32[316]{0:T(512)} %concatenate.9.info.refs_0_, bf16[8,128,128]{2,1,0:T(8,128)(2,1)} %copy-done.3, ...), custom_call_target="tpu_custom_call" | custom-call | flops 805306368 | bytes 14680064 | tf_op jit(solution)/shard_map/last/pallas_call | solution.py:777
  80.1 6.0 %all-to-all-start.3 = ((bf16[8,128,128]{2,1,0:T(8,128)(2,1)}), bf16[8,128,128]{2,1,0:T(8,128)(2,1)S(1)}, u32[]{:S(2)}, u32[]{:S(2)}) async-start(bf16[8,128,128]{2,1,0:T(8,128)(2,1)} %get-tuple-element.52), calls=%async_computation.3 | async-start | bytes 524288 | tf_op jit(solution)/shard_map/all_to_all | solution.py:722
  86.2 11.3 %spread.3 = (f32[32,128,128]{2,1,0:T(8,128)}, bf16[32,128,128]{2,1,0:T(8,128)(2,1)}, f32[8,128,128]{2,1,0:T(8,128)}, f32[8,128,128]{2,1,0:T(8,128)}) custom-call(s32[316]{0:T(512)} %concatenate.9.info.refs_0_, f32[72,128]{1,0:T(8,128)} %get-tuple-element.53.refs_1_.refs_6_.refs_2_, bf16[32,8,128,128]{3,2,1,0:T(8,128)(2,1)} %refs_3_.3, ...), custom_call_target="tpu_custom_call" | custom-call | flops 1073741824 | bytes 14680064 | tf_op jit(solution)/shard_map/spread/pallas_call | solution.py:781
  97.5 0.0 all-to-all-done.3.refs_1_
  97.5 0.0 copy-start.6
  97.6 0.7 copy-done.6
  98.2 4.2 %join.2 = (bf16[8,128,128]{2,1,0:T(8,128)(2,1)}, bf16[8,128,128]{2,1,0:T(8,128)(2,1)}, f32[8,128,128]{2,1,0:T(8,128)}) custom-call(s32[316]{0:T(512)} %concatenate.9.info.refs_0_, bf16[8,128,128]{2,1,0:T(8,128)(2,1)} %copy-done.6, f32[8,128,128]{2,1,0:T(8,128)} %get-tuple-element.57.refs_2_, f32[8,128,128]{2,1,0:T(8,128)} %get-tuple-element.58.refs_3_, ...), custom_call_target="tpu_custom_call" | custom-call | flops 100663296 | bytes 4194304 | tf_op jit(solution)/shard_map/join/pallas_call | solution.py:782
  102.4 6.0 %all-to-all-start.4 = ((bf16[8,128,128]{2,1,0:T(8,128)(2,1)}), bf16[8,128,128]{2,1,0:T(8,128)(2,1)S(1)}, u32[]{:S(2)}, u32[]{:S(2)}) async-start(bf16[8,128,128]{2,1,0:T(8,128)(2,1)} %get-tuple-element.61), calls=%async_computation.4 | async-start | bytes 524288 | tf_op jit(solution)/shard_map/all_to_all | solution.py:722
  108.5 12.2 %spread.4 = (f32[32,128,128]{2,1,0:T(8,128)}, bf16[32,128,128]{2,1,0:T(8,128)(2,1)}, f32[8,128,128]{2,1,0:T(8,128)}, f32[8,128,128]{2,1,0:T(8,128)}) custom-call(s32[316]{0:T(512)} %concatenate.9.info.refs_0_, bf16[8,128,128]{2,1,0:T(8,128)(2,1)} %get-tuple-element.62.refs_1_, f32[72,128]{1,0:T(8,128)} %get-tuple-element.53.refs_1_.refs_6_.refs_2_, ...), custom_call_target="tpu_custom_call" | custom-call | flops 1073741824 | bytes 14680064 | tf_op jit(solution)/shard_map/spread/pallas_call | solution.py:784
  120.7 0.0 all-to-all-done.4.refs_1_
  120.7 0.0 copy-start.5
  120.7 0.7 copy-done.5
  121.4 0.0 copy-start.1
  121.4 4.5 %join.3 = (bf16[8,128,128]{2,1,0:T(8,128)(2,1)}, bf16[8,128,128]{2,1,0:T(8,128)(2,1)}, f32[8,128,128]{2,1,0:T(8,128)}) custom-call(s32[316]{0:T(512)} %concatenate.9.info.refs_0_, bf16[8,128,128]{2,1,0:T(8,128)(2,1)} %copy-done.5, f32[8,128,128]{2,1,0:T(8,128)} %get-tuple-element.65.refs_2_, f32[8,128,128]{2,1,0:T(8,128)} %get-tuple-element.58.refs_3_, ...), custom_call_target="tpu_custom_call" | custom-call | flops 100663296 | bytes 4194304 | tf_op jit(solution)/shard_map/join/pallas_call | solution.py:787
  126.0 6.0 %all-to-all-start.5 = ((bf16[8,128,128]{2,1,0:T(8,128)(2,1)}), bf16[8,128,128]{2,1,0:T(8,128)(2,1)S(1)}, u32[]{:S(2)}, u32[]{:S(2)}) async-start(bf16[8,128,128]{2,1,0:T(8,128)(2,1)} %get-tuple-element.68), calls=%async_computation.5 | async-start | bytes 524288 | tf_op jit(solution)/shard_map/all_to_all | solution.py:722
  132.0 0.0 copy-done.1
  132.0 2.1 %select_reduce_fusion = f32[128]{0:T(128)S(1)} fusion(bf16[4096,128]{1,0:T(8,128)(2,1)S(1)} %copy-done.1, pred[4096]{0:T(1024)(128)(4,1)S(1)} %fusion.3), kind=kLoop, calls=%fused_computation | loop fusion | flops 1572736 | bytes 1053184 | tf_op jit(solution)/shard_map/reduce_sum | solution.py:795
  134.1 8.7 %spread.5 = (bf16[32,128,128]{2,1,0:T(8,128)(2,1)}, f32[8,128,128]{2,1,0:T(8,128)}) custom-call(s32[316]{0:T(512)} %concatenate.9.info.refs_0_, bf16[8,128,128]{2,1,0:T(8,128)(2,1)} %get-tuple-element.69.refs_1_, f32[72,128]{1,0:T(8,128)} %get-tuple-element.53.refs_1_.refs_6_.refs_2_, bf16[32,8,128,128]{3,2,1,0:T(8,128)(2,1)} %refs_3_.3, ...), custom_call_target="tpu_custom_call" | custom-call | flops 671088640 | bytes 14680064 | tf_op jit(solution)/shard_map/spread/pallas_call | solution.py:789
  142.9 0.0 all-to-all-done.5.got
  142.9 0.0 copy-start.4
  142.9 0.7 copy-done.4
  143.6 2.3 %close.1 = bf16[32,128,128]{2,1,0:T(8,128)(2,1)} custom-call(s32[316]{0:T(512)} %concatenate.9.info.refs_0_, bf16[8,128,128]{2,1,0:T(8,128)(2,1)} %copy-done.4, f32[8,128,128]{2,1,0:T(8,128)} %get-tuple-element.72.totl, bf16[8,128,128]{2,1,0:T(8,128)(2,1)} %get-tuple-element.59.refs_4_.wl, ...), custom_call_target="tpu_custom_call", output_to_operand_aliasing={{}: (5, {})} | custom-call | flops 16384 | bytes 2097152 | tf_op jit(solution)/shard_map/close/pallas_call | solution.py:790
  145.9 1.5 convolution_bitcast_fusion
  147.4 13.4 %all_to_all.40 = f32[8,40,128]{2,1,0:T(8,128)S(1)} all-to-all(f32[8,40,128]{2,1,0:T(8,128)S(1)} %broadcast_in_dim.24), channel_id=1, replica_groups=mesh['grp'=4,'dom'=8] {'dom'}, dimensions={0} | all-to-all | bytes 327680 | tf_op jit(solution)/shard_map/all_to_all | solution.py:722
  160.8 6.8 %all_to_all.41 = f32[4,40,128]{2,1,0:T(8,128)S(1)} all-to-all(f32[4,40,128]{2,1,0:T(8,128)S(1)} %broadcast_in_dim.25), channel_id=1, replica_groups=mesh['grp'=4,'dom'=8] {'grp'}, dimensions={0} | all-to-all | bytes 163840 | tf_op jit(solution)/shard_map/all_to_all | solution.py:722
  167.7 0.6 slice_divide_fusion
  (11 shorter events, 0.1 us)
Async XLA Ops:
  0.6 13.9 %copy-start = (bf16[32,4096]{1,0:T(8,128)(2,1)S(1)}, bf16[32,4096]{1,0:T(8,128)(2,1)}, u32[]{:S(2)}) copy-start(bf16[32,4096]{1,0:T(8,128)(2,1)} %param.12) | copy-start | bytes 786436
  7.3 16.9 %all-to-all-start = ((bf16[8,144,128]{2,1,0:T(8,128)(2,1)}), bf16[8,144,128]{2,1,0:T(8,128)(2,1)S(1)}, u32[]{:S(2)}, u32[]{:S(2)}) async-start(bf16[8,144,128]{2,1,0:T(8,128)(2,1)} %pack.1), calls=%async_computation | async-start | bytes 589824 | tf_op jit(solution)/shard_map/all_to_all | solution.py:722
  24.2 0.7 copy-start.2
  34.5 14.7 %all-to-all-start.1 = ((bf16[8,128,128]{2,1,0:T(8,128)(2,1)}), bf16[8,128,128]{2,1,0:T(8,128)(2,1)S(1)}, u32[]{:S(2)}, u32[]{:S(2)}) async-start(bf16[8,128,128]{2,1,0:T(8,128)(2,1)} %get-tuple-element.40), calls=%async_computation.1 | async-start | bytes 524288 | tf_op jit(solution)/shard_map/all_to_all | solution.py:722
  49.2 0.7 copy-start.7
  53.5 16.9 %all-to-all-start.2 = ((bf16[8,128,128]{2,1,0:T(8,128)(2,1)}), bf16[8,128,128]{2,1,0:T(8,128)(2,1)S(1)}, u32[]{:S(2)}, u32[]{:S(2)}) async-start(bf16[8,128,128]{2,1,0:T(8,128)(2,1)} %get-tuple-element.44), calls=%async_computation.2 | async-start | bytes 524288 | tf_op jit(solution)/shard_map/all_to_all | solution.py:722
  70.5 0.7 copy-start.3
  80.1 17.4 %all-to-all-start.3 = ((bf16[8,128,128]{2,1,0:T(8,128)(2,1)}), bf16[8,128,128]{2,1,0:T(8,128)(2,1)S(1)}, u32[]{:S(2)}, u32[]{:S(2)}) async-start(bf16[8,128,128]{2,1,0:T(8,128)(2,1)} %get-tuple-element.52), calls=%async_computation.3 | async-start | bytes 524288 | tf_op jit(solution)/shard_map/all_to_all | solution.py:722
  97.5 0.7 copy-start.6
  102.4 18.2 %all-to-all-start.4 = ((bf16[8,128,128]{2,1,0:T(8,128)(2,1)}), bf16[8,128,128]{2,1,0:T(8,128)(2,1)S(1)}, u32[]{:S(2)}, u32[]{:S(2)}) async-start(bf16[8,128,128]{2,1,0:T(8,128)(2,1)} %get-tuple-element.61), calls=%async_computation.4 | async-start | bytes 524288 | tf_op jit(solution)/shard_map/all_to_all | solution.py:722
  120.7 0.7 copy-start.5
  121.4 10.6 %copy-start.1 = (bf16[4096,128]{1,0:T(8,128)(2,1)S(1)}, bf16[4096,128]{1,0:T(8,128)(2,1)}, u32[]{:S(2)}) copy-start(bf16[4096,128]{1,0:T(8,128)(2,1)} %param.19) | copy-start | bytes 3145732
  126.0 16.9 %all-to-all-start.5 = ((bf16[8,128,128]{2,1,0:T(8,128)(2,1)}), bf16[8,128,128]{2,1,0:T(8,128)(2,1)S(1)}, u32[]{:S(2)}, u32[]{:S(2)}) async-start(bf16[8,128,128]{2,1,0:T(8,128)(2,1)} %get-tuple-element.68), calls=%async_computation.5 | async-start | bytes 524288 | tf_op jit(solution)/shard_map/all_to_all | solution.py:722
  142.9 0.7 copy-start.4
